TPU v7x, 256 devices: a whole 4x4x8 slice. The times are simulated.
256 devices in a mesh: space: 128 (over z, y, x), rep: 2 (over core).
Axes of the slice: x: 4, y: 4, z: 8, core: 2. Of those that a mesh axis runs over, the one named last changes fastest.
Arguments:
- features: bfloat16 [2, 512, 64, 512], P('rep', 'space'), may hold values from -6 to 6
- neighbours: int32 [2, 512, 26], P('rep', 'space'), may hold values from -1 to 35, as said below
- send_list: int32 [2, 128, 2, 16], P('rep', 'space'), may hold values from -1 to 3, as said below
- w_fine: bfloat16 [64, 1728], replicated, may hold values from -0.15625 to 0.15625
- w_down: bfloat16 [64, 512], replicated, may hold values from -0.25 to 0.25
- w_coarse: bfloat16 [64, 1728], replicated, may hold values from -0.15625 to 0.15625
- w_up: bfloat16 [64, 512], replicated, may hold values from -0.75 to 0.75
- cotangent: bfloat16 [2, 512, 64, 512], P('rep', 'space'), may hold values from -6 to 6
Outputs:
- decoded: bfloat16 [2, 512, 64, 512], P('rep', 'space')
- grad_fine: float32 [64, 1728], replicated
- grad_down: float32 [64, 512], replicated
- grad_coarse: float32 [64, 1728], replicated
- grad_up: float32 [64, 512], replicated
Inputs may be any that keep to these rules, and one draw needn't show every extreme that they name: `neighbours`: A scene is a corridor 4 block positions across in the second and third dimensions; device d holds the occupied positions whose first coordinate lies in 4 d .. 4 d + 3, in Morton order. Entries follow true adjacency: below 4 a block of the same device, 4 + s (s < 4**2) the block of device d - 1 in slot s of its side 0, 4 + 4**2 + s the block of device d + 1 in slot s of its side 1, -1 an empty or outside position. In every slab the positions (0, 3, 3) and (3, 3, 3) are occupied and (3, 0, 0) is empty. send_list[d, 0, y * 4 + z] is device d's block at the last first-coordinate plane of its slab and position (y, z), send_list[d, 1, y * 4 + z] the one at the first plane; -1 where that position is empty.
All inputs are finite; a program needn't handle non-finite values.
Results may differ from a plain program's by a relative error of at most 0.007.
Values may be sent and summed in bfloat16 or wider, within the bound.
No kernel may reach another device: no remote copies, remote signals or barrier semaphores. Data moves between devices by JAX's collectives and lax.ppermute only.
A program may use at most 128 MiB of HBM per device.

v0:
```python
import math
import jax
import jax.numpy as jnp
from jax import lax
from jax.sharding import PartitionSpec as P

EDGE = 8
DIRECTIONS = [
    (a, c, e) for a in (-1, 0, 1) for c in (-1, 0, 1) for e in (-1, 0, 1) if (a, c, e) != (0, 0, 0)
]


def passed_along(block, axis, distance):
    devices = range(lax.axis_size(axis))
    route = [(i - distance, i) for i in devices if i - distance in devices]
    return lax.ppermute(block, axis, route)


def silu_slope(values):
    sig = jax.nn.sigmoid(values)
    return sig * (1.0 + values * (1.0 - sig))


def source_range(step, side):
    if step < 0:
        return slice(side - 1, side)
    if step == 0:
        return slice(0, side)
    return slice(0, 1)


def target_range(step, side):
    if step < 0:
        return slice(0, 1)
    if step == 0:
        return slice(1, side + 1)
    return slice(side + 1, side + 2)


def assemble(own_blocks, combined, sources, side):
    count, channels = (own_blocks.shape[0], own_blocks.shape[1])
    cubes = combined.reshape(combined.shape[0], channels, side, side, side)
    padded = jnp.zeros((count, channels, side + 2, side + 2, side + 2), own_blocks.dtype)
    padded = padded.at[:, :, 1 : side + 1, 1 : side + 1, 1 : side + 1].set(
        own_blocks.reshape(count, channels, side, side, side)
    )
    for k, (a, c, e) in enumerate(DIRECTIONS):
        part_cells = cubes[
            :, :, source_range(a, side), source_range(c, side), source_range(e, side)
        ]
        source_ids = sources[:, k]
        gathered = jnp.take(part_cells, jnp.maximum(source_ids, 0), axis=0)
        gathered = jnp.where(
            (source_ids >= 0)[:, None, None, None, None], gathered, jnp.zeros_like(gathered)
        )
        padded = padded.at[
            :, :, target_range(a, side), target_range(c, side), target_range(e, side)
        ].set(gathered)
    return padded


def lattice_columns(padded, side):
    count, channels = (padded.shape[0], padded.shape[1])
    parts_list = [
        padded[:, :, a : a + side, c : c + side, e : e + side].reshape(count, channels, side**3)
        for a in range(3)
        for c in range(3)
        for e in range(3)
    ]
    return jnp.concatenate(parts_list, axis=1)


def spread_back(back_cols, side):
    count = back_cols.shape[0]
    channels = back_cols.shape[1] // 27
    result = jnp.zeros((count, channels, side + 2, side + 2, side + 2), jnp.float32)
    for a in range(3):
        for c in range(3):
            for e in range(3):
                offset = 9 * a + 3 * c + e
                piece = back_cols[:, offset * channels : (offset + 1) * channels].reshape(
                    count, channels, side, side, side
                )
                result = result.at[:, :, a : a + side, c : c + side, e : e + side].add(piece)
    return result


def to_patches(field, side):
    count, channels = (field.shape[0], field.shape[1])
    half = side // 2
    shaped = field.reshape(count, channels, half, 2, half, 2, half, 2).transpose(
        0, 3, 5, 7, 1, 2, 4, 6
    )
    return shaped.reshape(count, 8 * channels, half**3)


def from_patches(values, half):
    count = values.shape[0]
    channels = values.shape[1] // 8
    shaped = values.reshape(count, 2, 2, 2, channels, half, half, half).transpose(
        0, 4, 5, 1, 6, 2, 7, 3
    )
    return shaped.reshape(count, channels, 8 * half**3)


def shards(features, neighbours, send_list, w_fine, w_down, w_coarse, w_up, cotangent):
    f32 = jnp.float32
    fine_in = features[0]
    sources = neighbours[0]
    sends = send_list[0, 0]
    block_count, channels = (fine_in.shape[0], fine_in.shape[1])
    slot_count = sends.shape[1]
    peer_count = lax.axis_size("space")
    coarse_side = EDGE // 2
    upper_ids = jnp.maximum(sends[0], 0)
    lower_ids = jnp.maximum(sends[1], 0)
    to_upper = jnp.take(fine_in, upper_ids, axis=0)
    to_lower = jnp.take(fine_in, lower_ids, axis=0)
    arrived = []
    for offset, payload in ((1, to_upper), (-1, to_lower)):
        arrived.append(passed_along(payload, "space", offset))
    halo0 = assemble(fine_in, jnp.concatenate([fine_in] + arrived, axis=0), sources, EDGE)
    pad_groups = halo0.reshape((block_count // 4, 4) + halo0.shape[1:])

    def fine_forward(pad_group):
        return jnp.einsum(
            "ok,gkv->gov", w_fine, lattice_columns(pad_group, EDGE), preferred_element_type=f32
        )

    fine_pre = lax.map(fine_forward, pad_groups).reshape(block_count, channels, EDGE**3)
    hidden0 = jax.nn.silu(fine_pre).astype(jnp.bfloat16)
    patches0 = to_patches(hidden0, EDGE)
    coarse_pre = jnp.einsum("ok,bkv->bov", w_down, patches0, preferred_element_type=f32)
    hidden1 = jax.nn.silu(coarse_pre).astype(jnp.bfloat16)
    coarse_upper = jnp.take(hidden1, upper_ids, axis=0)
    coarse_lower = jnp.take(hidden1, lower_ids, axis=0)
    arrived1 = []
    for offset, payload in ((1, coarse_upper), (-1, coarse_lower)):
        arrived1.append(passed_along(payload, "space", offset))
    halo1 = assemble(hidden1, jnp.concatenate([hidden1] + arrived1, axis=0), sources, coarse_side)
    columns1 = lattice_columns(halo1, coarse_side)
    coarse_conv = jnp.einsum("ok,bkv->bov", w_coarse, columns1, preferred_element_type=f32)
    gated = jax.nn.silu(coarse_conv).astype(jnp.bfloat16)
    up_terms = from_patches(
        jnp.einsum("ik,biv->bkv", w_up, gated, preferred_element_type=f32), coarse_side
    )
    decoded = (hidden0.astype(f32) + up_terms).astype(jnp.bfloat16)
    cot_patch = to_patches(cotangent[0], EDGE)
    grad_up = jnp.einsum("biv,bkv->ik", gated, cot_patch, preferred_element_type=f32)
    up_back = jnp.einsum("ik,bkv->biv", w_up, cot_patch, preferred_element_type=f32)
    delta_up = (up_back * silu_slope(coarse_conv)).astype(jnp.bfloat16)
    grad_coarse = jnp.einsum("bov,bkv->ok", delta_up, columns1, preferred_element_type=f32)
    back_cols = jnp.einsum("ok,bov->bkv", w_coarse, delta_up, preferred_element_type=f32)
    back_pad = spread_back(back_cols, coarse_side)
    slot_total = block_count + 2 * slot_count
    slot_ids = jnp.arange(slot_total, dtype=jnp.int32)
    accumulated = jnp.zeros((slot_total, channels, coarse_side, coarse_side, coarse_side), f32)
    for k, (a, c, e) in enumerate(DIRECTIONS):
        piece = back_pad[
            :,
            :,
            target_range(a, coarse_side),
            target_range(c, coarse_side),
            target_range(e, coarse_side),
        ]
        selector = (sources[:, k][:, None] == slot_ids[None, :]).astype(f32)
        moved = jnp.einsum("bm,bcxyz->mcxyz", selector, piece, precision=lax.Precision.HIGHEST)
        accumulated = accumulated.at[
            :,
            :,
            source_range(a, coarse_side),
            source_range(c, coarse_side),
            source_range(e, coarse_side),
        ].add(moved)
    lower_owned = accumulated[block_count : block_count + slot_count][
        :, :, coarse_side - 1
    ].reshape(slot_count, channels * coarse_side**2)
    upper_owned = accumulated[block_count + slot_count :][:, :, 0].reshape(
        slot_count, channels * coarse_side**2
    )
    returned = []
    for offset, payload in ((-1, lower_owned), (1, upper_owned)):
        returned.append(
            passed_along(payload.astype(jnp.bfloat16), "space", offset).astype(payload.dtype)
        )
    block_ids = jnp.arange(block_count, dtype=jnp.int32)
    chooser_upper = (sends[0][:, None] == block_ids[None, :]).astype(f32)
    chooser_lower = (sends[1][:, None] == block_ids[None, :]).astype(f32)
    face_high = jnp.einsum("sb,sf->bf", chooser_upper, returned[0], precision=lax.Precision.HIGHEST)
    face_low = jnp.einsum("sb,sf->bf", chooser_lower, returned[1], precision=lax.Precision.HIGHEST)
    centre = back_pad[:, :, 1 : coarse_side + 1, 1 : coarse_side + 1, 1 : coarse_side + 1]
    grad_cube = centre + accumulated[:block_count]
    grad_cube = grad_cube.at[:, :, coarse_side - 1].add(
        face_high.reshape(block_count, channels, coarse_side, coarse_side)
    )
    grad_cube = grad_cube.at[:, :, 0].add(
        face_low.reshape(block_count, channels, coarse_side, coarse_side)
    )
    grad_hidden1 = grad_cube.reshape(block_count, channels, coarse_side**3)
    delta_down = (grad_hidden1 * silu_slope(coarse_pre)).astype(jnp.bfloat16)
    grad_down = jnp.einsum("bov,bkv->ok", delta_down, patches0, preferred_element_type=f32)
    down_back = jnp.einsum("ok,bov->bkv", w_down, delta_down, preferred_element_type=f32)
    grad_hidden0 = cotangent[0].astype(f32) + from_patches(down_back, coarse_side)
    delta_fine = (grad_hidden0 * silu_slope(fine_pre)).astype(jnp.bfloat16)
    delta_groups = delta_fine.reshape((block_count // 4, 4) + delta_fine.shape[1:])

    def fine_weights(total, pair):
        pad_group, delta_group = pair
        cols = lattice_columns(pad_group, EDGE)
        return (
            total + jnp.einsum("gov,gkv->ok", delta_group, cols, preferred_element_type=f32),
            None,
        )

    grad_fine, _ = lax.scan(fine_weights, jnp.zeros(w_fine.shape, f32), (pad_groups, delta_groups))
    grad_fine, grad_down, grad_coarse, grad_up = lax.psum(
        (grad_fine, grad_down, grad_coarse, grad_up), ("space", "rep")
    )
    factor = 1.0 / math.sqrt(lax.axis_size("rep") * peer_count * block_count * EDGE**3)
    return (
        decoded[None],
        grad_fine * factor,
        grad_down * factor,
        grad_coarse * factor,
        grad_up * factor,
    )


def solution(mesh):
    in_specs = (
        P("rep", "space", None, None),
        P("rep", "space", None),
        P("rep", "space", None, None),
        P(),
        P(),
        P(),
        P(),
        P("rep", "space", None, None),
    )
    out_specs = (P("rep", "space", None, None), P(), P(), P(), P())
    return jax.shard_map(shards, mesh=mesh, in_specs=in_specs, out_specs=out_specs, check_vma=False)
```

profile of v0, /device:TPU:2, one launch (start us, length us, event | category | flops | bytes accessed | tf_op | source)
XLA Modules:
  0.0 604.1 jit_solution(300199098272582646)
XLA Ops:
  8.8 1.6 gather_fusion
  10.6 3.4 collective-permute-start
  15.8 3.4 collective-permute-start.1
  43.3 2.0 concatenate.387
  48.4 3.0 copy.303
  51.4 3.8 copy.304
  58.0 2.5 pad_maximum_fusion
  94.1 1.7 gather_fusion.17
  105.1 3.2 fusion.228
  108.3 5.6 fusion.227
  113.9 2.1 copy.375
  116.0 2.0 copy.374
  118.0 2.0 copy.373
  120.0 2.0 copy.372
  123.0 2.1 copy.370
  125.1 2.0 copy.369
  130.4 2.0 copy.393
  133.4 2.1 copy.391
  135.5 2.0 copy.390
  137.5 2.0 copy.389
  139.5 2.0 copy.388
  141.5 2.0 copy.387
  144.6 2.1 copy.385
  146.6 2.0 copy.384
  148.6 2.0 copy.383
  150.6 2.0 copy.382
  152.7 2.0 copy.381
  158.3 1.7 constant_dynamic-update-slice_fusion.25
  160.0 1.7 constant_dynamic-update-slice_fusion.24
  161.8 1.7 constant_dynamic-update-slice_fusion.23
  180.5 4.4 multiply_convert_fusion
  189.4 2.4 collective-permute-start.2
  191.9 4.1 collective-permute-start.3
  199.2 2.1 collective-permute-done.3
  261.2 3.1 concatenate.384
  268.8 2.0 fusion.80
  280.3 2.3 fusion.22
  283.7 2.3 fusion.27
  286.3 2.2 fusion.30
  290.6 5.0 collective-permute-start.5
  296.7 2.2 collective-permute-start.4
  300.9 6.0 collective-permute-done.4
  311.8 6.0 convolution_bitcast_fusion.2
  320.4 269.7 %all-reduce.7.cloned.1.call-done = (f32[64,1728]{1,0:T(8,128)}, f32[64,512]{1,0:T(8,128)}, f32[64,1728]{1,0:T(8,128)}, f32[64,512]{1,0:T(8,128)}) async-done(((f32[64,1728]{1,0:T(8,128)}, f32[64,512]{1,0:T(8,128)}, f32[64,1728]{1,0:T(8,128)}, f32[64,512]{1,0:T(8,128)}), (f32[64,1728]{1,0:T(8,128)}, f32[64,512]{1,0:T(8,128)}, f32[64,1728]{1,0:T(8,128)}, f32[64,512]{1,0:T(8,128)})) %all-reduce.7.cloned.1.call-update) | async-done | bytes 1146896 | tf_op jit(solution)/shard_map/psum | solution.py:216
  590.0 1.8 broadcast_multiply_fusion.1
  591.9 1.6 broadcast_multiply_fusion.3
  593.4 1.6 broadcast_multiply_fusion.2
  595.0 1.8 broadcast_multiply_fusion
  (731 shorter events, 196.5 us)
Async XLA Ops:
  7.2 257.1 %copy-start = (bf16[64,1728]{1,0:T(8,128)(2,1)S(1)}, bf16[64,1728]{1,0:T(8,128)(2,1)}, u32[]{:S(2)}) copy-start(bf16[64,1728]{1,0:T(8,128)(2,1)} %param.261) | copy-start | bytes 663556
  7.2 582.9 %all-reduce.7.cloned.1.call-start = ((), (), s32[]{:S(2)}) async-start(), calls=%async_computation | async-start | bytes 2359296 | tf_op jit(solution)/shard_map/psum | solution.py:216
  10.6 37.8 %collective-permute-start = (bf16[16,64,512]{2,1,0:T(8,128)(2,1)S(1)}, bf16[16,64,512]{2,1,0:T(8,128)(2,1)}, u32[]{:S(2)}, u32[]{:S(2)}) collective-permute-start(bf16[16,64,512]{2,1,0:T(8,128)(2,1)S(1)} %broadcast_select_fusion.1), channel_id=1, source_target_pairs={{0,2},{2,4},{4,6},{6,8},{8,10},{10,12},{12,14},{14,16},{16,18},{18... | collective-permute-start | bytes 3145736 | tf_op jit(solution)/shard_map/ppermute | solution.py:16
  15.8 35.5 %collective-permute-start.1 = (bf16[16,64,512]{2,1,0:T(8,128)(2,1)}, bf16[16,64,512]{2,1,0:T(8,128)(2,1)}, u32[]{:S(2)}, u32[]{:S(2)}) collective-permute-start(bf16[16,64,512]{2,1,0:T(8,128)(2,1)} %broadcast_select_fusion), channel_id=1, source_target_pairs={{2,0},{4,2},{6,4},{8,6},{10,8},{12,10},{14,12},{16,14},{18,16},{20... | collective-permute-start | bytes 3145736 | tf_op jit(solution)/shard_map/ppermute | solution.py:16
  19.3 22.6 %copy-start.150 = (s32[2]{0:T(128)}, s32[2]{0:T(128)S(1)}, u32[]{:S(2)}) copy-start(s32[2]{0:T(128)S(1)} %iota_multiply_fusion) | copy-start | bytes 28
  20.2 21.6 %copy-start.73 = (s32[4]{0:T(128)}, s32[4]{0:T(128)S(1)}, u32[]{:S(2)}) copy-start(s32[4]{0:T(128)S(1)} %get-tuple-element.1376) | copy-start | bytes 52
  23.2 18.7 %copy-start.43 = (s32[4]{0:T(128)}, s32[4]{0:T(128)S(1)}, u32[]{:S(2)}) copy-start(s32[4]{0:T(128)S(1)} %get-tuple-element.1356) | copy-start | bytes 52
  23.2 18.7 %copy-start.45 = (s32[4]{0:T(128)}, s32[4]{0:T(128)S(1)}, u32[]{:S(2)}) copy-start(s32[4]{0:T(128)S(1)} %get-tuple-element.1357) | copy-start | bytes 52
  23.2 18.7 %copy-start.47 = (s32[4]{0:T(128)}, s32[4]{0:T(128)S(1)}, u32[]{:S(2)}) copy-start(s32[4]{0:T(128)S(1)} %get-tuple-element.1359) | copy-start | bytes 52
  23.2 18.7 %copy-start.49 = (s32[4]{0:T(128)}, s32[4]{0:T(128)S(1)}, u32[]{:S(2)}) copy-start(s32[4]{0:T(128)S(1)} %get-tuple-element.1361) | copy-start | bytes 52
  23.2 18.7 %copy-start.107 = (s32[4]{0:T(128)}, s32[4]{0:T(128)S(1)}, u32[]{:S(2)}) copy-start(s32[4]{0:T(128)S(1)} %get-tuple-element.1352) | copy-start | bytes 52
  23.2 18.7 %copy-start.109 = (s32[4]{0:T(128)}, s32[4]{0:T(128)S(1)}, u32[]{:S(2)}) copy-start(s32[4]{0:T(128)S(1)} %get-tuple-element.1354) | copy-start | bytes 52
  23.3 18.7 %copy-start.111 = (s32[4]{0:T(128)}, s32[4]{0:T(128)S(1)}, u32[]{:S(2)}) copy-start(s32[4]{0:T(128)S(1)} %get-tuple-element.1358) | copy-start | bytes 52
  23.3 18.7 %copy-start.113 = (s32[4]{0:T(128)}, s32[4]{0:T(128)S(1)}, u32[]{:S(2)}) copy-start(s32[4]{0:T(128)S(1)} %get-tuple-element.1360) | copy-start | bytes 52
  23.3 25.0 %copy-start.51 = (s32[4]{0:T(128)}, s32[4]{0:T(128)S(1)}, u32[]{:S(2)}) copy-start(s32[4]{0:T(128)S(1)} %get-tuple-element.1362) | copy-start | bytes 52
  23.3 25.0 %copy-start.53 = (s32[4]{0:T(128)}, s32[4]{0:T(128)S(1)}, u32[]{:S(2)}) copy-start(s32[4]{0:T(128)S(1)} %get-tuple-element.1363) | copy-start | bytes 52
  23.3 25.0 %copy-start.55 = (s32[4]{0:T(128)}, s32[4]{0:T(128)S(1)}, u32[]{:S(2)}) copy-start(s32[4]{0:T(128)S(1)} %get-tuple-element.1364) | copy-start | bytes 52
  23.3 25.0 %copy-start.57 = (s32[4]{0:T(128)}, s32[4]{0:T(128)S(1)}, u32[]{:S(2)}) copy-start(s32[4]{0:T(128)S(1)} %get-tuple-element.1365) | copy-start | bytes 52
  23.3 25.0 %copy-start.59 = (s32[4]{0:T(128)}, s32[4]{0:T(128)S(1)}, u32[]{:S(2)}) copy-start(s32[4]{0:T(128)S(1)} %get-tuple-element.1366) | copy-start | bytes 52
  23.3 25.0 %copy-start.61 = (s32[4]{0:T(128)}, s32[4]{0:T(128)S(1)}, u32[]{:S(2)}) copy-start(s32[4]{0:T(128)S(1)} %get-tuple-element.1367) | copy-start | bytes 52
  23.3 25.0 %copy-start.63 = (s32[4]{0:T(128)}, s32[4]{0:T(128)S(1)}, u32[]{:S(2)}) copy-start(s32[4]{0:T(128)S(1)} %get-tuple-element.1368) | copy-start | bytes 52
  23.3 25.0 %copy-start.115 = (s32[4]{0:T(128)}, s32[4]{0:T(128)S(1)}, u32[]{:S(2)}) copy-start(s32[4]{0:T(128)S(1)} %get-tuple-element.1369) | copy-start | bytes 52
  94.1 10.2 %copy-start.134 = (pred[4]{0:T(512)(128)(4,1)S(1)}, pred[4]{0:T(512)(128)(4,1)}, u32[]{:S(2)}) copy-start(pred[4]{0:T(512)(128)(4,1)} %get-tuple-element.1592) | copy-start | bytes 16
  94.1 10.2 %copy-start.135 = (pred[4]{0:T(512)(128)(4,1)S(1)}, pred[4]{0:T(512)(128)(4,1)}, u32[]{:S(2)}) copy-start(pred[4]{0:T(512)(128)(4,1)} %get-tuple-element.1593) | copy-start | bytes 16
  133.4 10.1 %copy-start.8 = (bf16[4,64,8,8,8]{1,0,4,3,2:T(4,128)(2,1)S(1)}, bf16[4,64,8,8,8]{1,0,4,3,2:T(4,128)(2,1)}, u32[]{:S(2)}) copy-start(bf16[4,64,8,8,8]{1,0,4,3,2:T(4,128)(2,1)} %get-tuple-element.1447) | copy-start | bytes 786436
  144.6 10.1 %copy-start.7 = (bf16[4,64,8,8,8]{1,0,4,3,2:T(4,128)(2,1)S(1)}, bf16[4,64,8,8,8]{1,0,4,3,2:T(4,128)(2,1)}, u32[]{:S(2)}) copy-start(bf16[4,64,8,8,8]{1,0,4,3,2:T(4,128)(2,1)} %get-tuple-element.1453) | copy-start | bytes 786436
  185.6 10.3 %copy-start.158 = (s32[5]{0:T(128)S(1)}, s32[5]{0:T(128)}, u32[]{:S(2)}) copy-start(s32[5]{0:T(128)} %concatenate.387) | copy-start | bytes 64
  185.6 10.3 %copy-start.159 = (s32[5]{0:T(128)S(1)}, s32[5]{0:T(128)}, u32[]{:S(2)}) copy-start(s32[5]{0:T(128)} %constant.3474.clone.1) | copy-start | bytes 64
  185.7 10.9 %copy-start.12 = (bf16[1,4,64,512]{3,2,1,0:T(8,128)(2,1)S(1)}, bf16[1,4,64,512]{3,2,1,0:T(8,128)(2,1)}, u32[]{:S(2)}) copy-start(bf16[1,4,64,512]{3,2,1,0:T(8,128)(2,1)} %param.263) | copy-start | bytes 786436
  187.6 10.7 %copy-start.151 = (s32[2]{0:T(128)S(1)}, s32[2]{0:T(128)}, u32[]{:S(2)}) copy-start(s32[2]{0:T(128)} %copy-done.150) | copy-start | bytes 28
  187.6 10.7 %copy-start.156 = (s32[5]{0:T(128)S(1)}, s32[5]{0:T(128)}, u32[]{:S(2)}) copy-start(s32[5]{0:T(128)} %constant.3473.clone.1) | copy-start | bytes 64
  187.6 10.7 %copy-start.157 = (s32[5]{0:T(128)S(1)}, s32[5]{0:T(128)}, u32[]{:S(2)}) copy-start(s32[5]{0:T(128)} %constant.3471.clone.1) | copy-start | bytes 64
  189.4 9.8 %collective-permute-start.2 = (bf16[16,64,64]{1,2,0:T(8,128)(2,1)S(1)}, bf16[16,64,64]{1,2,0:T(8,128)(2,1)}, u32[]{:S(2)}, u32[]{:S(2)}) collective-permute-start(bf16[16,64,64]{1,2,0:T(8,128)(2,1)S(1)} %broadcast_select_fusion.3), channel_id=1, source_target_pairs={{0,2},{2,4},{4,6},{6,8},{8,10},{10,12},{12,14},{14,16},{16,18},{18... | collective-permute-start | bytes 393224 | tf_op jit(solution)/shard_map/ppermute | solution.py:16
  191.9 9.4 %collective-permute-start.3 = (bf16[16,64,64]{1,2,0:T(8,128)(2,1)}, bf16[16,64,64]{1,2,0:T(8,128)(2,1)}, u32[]{:S(2)}, u32[]{:S(2)}) collective-permute-start(bf16[16,64,64]{1,2,0:T(8,128)(2,1)} %broadcast_select_fusion.2), channel_id=1, source_target_pairs={{2,0},{4,2},{6,4},{8,6},{10,8},{12,10},{14,12},{16,14},{18,16},{20... | collective-permute-start | bytes 393224 | tf_op jit(solution)/shard_map/ppermute | solution.py:16
  203.2 17.0 %copy-start.153 = (pred[4]{0:T(512)(128)(4,1)S(1)}, pred[4]{0:T(512)(128)(4,1)}, u32[]{:S(2)}) copy-start(pred[4]{0:T(512)(128)(4,1)} %get-tuple-element.1629) | copy-start | bytes 16
  204.7 36.3 %copy-start.122 = (pred[4]{0:T(512)(128)(4,1)S(1)}, pred[4]{0:T(512)(128)(4,1)}, u32[]{:S(2)}) copy-start(pred[4]{0:T(512)(128)(4,1)} %get-tuple-element.1572) | copy-start | bytes 16
  204.9 37.5 %copy-start.118 = (pred[4]{0:T(512)(128)(4,1)S(1)}, pred[4]{0:T(512)(128)(4,1)}, u32[]{:S(2)}) copy-start(pred[4]{0:T(512)(128)(4,1)} %get-tuple-element.1576) | copy-start | bytes 16
  205.0 37.5 %copy-start.120 = (pred[4]{0:T(512)(128)(4,1)S(1)}, pred[4]{0:T(512)(128)(4,1)}, u32[]{:S(2)}) copy-start(pred[4]{0:T(512)(128)(4,1)} %get-tuple-element.1577) | copy-start | bytes 16
  241.8 13.4 %copy-start.96 = (pred[4]{0:T(512)(128)(4,1)S(1)}, pred[4]{0:T(512)(128)(4,1)}, u32[]{:S(2)}) copy-start(pred[4]{0:T(512)(128)(4,1)} %get-tuple-element.1556) | copy-start | bytes 16
  241.8 13.4 %copy-start.98 = (pred[4]{0:T(512)(128)(4,1)S(1)}, pred[4]{0:T(512)(128)(4,1)}, u32[]{:S(2)}) copy-start(pred[4]{0:T(512)(128)(4,1)} %get-tuple-element.1557) | copy-start | bytes 16
  244.1 11.9 %copy-start.86 = (pred[4]{0:T(512)(128)(4,1)S(1)}, pred[4]{0:T(512)(128)(4,1)}, u32[]{:S(2)}) copy-start(pred[4]{0:T(512)(128)(4,1)} %get-tuple-element.1632) | copy-start | bytes 16
  244.1 11.9 %copy-start.88 = (pred[4]{0:T(512)(128)(4,1)S(1)}, pred[4]{0:T(512)(128)(4,1)}, u32[]{:S(2)}) copy-start(pred[4]{0:T(512)(128)(4,1)} %get-tuple-element.1633) | copy-start | bytes 16
  280.3 9.6 %copy-start.108 = (s32[4]{0:T(128)S(1)}, s32[4]{0:T(128)}, u32[]{:S(2)}) copy-start(s32[4]{0:T(128)} %copy-done.107) | copy-start | bytes 52
  289.8 9.8 %copy-start.155 = (s32[16]{0:T(128)S(1)}, s32[16]{0:T(128)}, u32[]{:S(2)}) copy-start(s32[16]{0:T(128)} %get-tuple-element.1521) | copy-start | bytes 196
  290.2 16.6 %copy-start.154 = (s32[16]{0:T(128)S(1)}, s32[16]{0:T(128)}, u32[]{:S(2)}) copy-start(s32[16]{0:T(128)} %get-tuple-element.1522) | copy-start | bytes 196
  290.6 9.0 %collective-permute-start.5 = (bf16[16,1024]{0,1:T(8,128)(2,1)S(1)}, bf16[16,1024]{0,1:T(8,128)(2,1)S(1)}, u32[]{:S(2)}, u32[]{:S(2)}) collective-permute-start(bf16[16,1024]{0,1:T(8,128)(2,1)S(1)} %bitcast.1005), channel_id=1, source_target_pairs={{0,2},{2,4},{4,6},{6,8},{8,10},{10,12},{12,14},{14,16},{16,18},{18... | collective-permute-start | bytes 98312 | tf_op jit(solution)/shard_map/ppermute | solution.py:16
  296.5 13.5 %copy-start.36 = (bf16[64,512]{1,0:T(8,128)(2,1)S(1)}, bf16[64,512]{1,0:T(8,128)(2,1)}, u32[]{:S(2)}) copy-start(bf16[64,512]{1,0:T(8,128)(2,1)} %param.260) | copy-start | bytes 196612
  296.7 10.1 %collective-permute-start.4 = (bf16[16,1024]{0,1:T(8,128)(2,1)S(1)}, bf16[16,1024]{0,1:T(8,128)(2,1)S(1)}, u32[]{:S(2)}, u32[]{:S(2)}) collective-permute-start(bf16[16,1024]{0,1:T(8,128)(2,1)S(1)} %bitcast.1004), channel_id=1, source_target_pairs={{2,0},{4,2},{6,4},{8,6},{10,8},{12,10},{14,12},{16,14},{18,16},{20... | collective-permute-start | bytes 98312 | tf_op jit(solution)/shard_map/ppermute | solution.py:16
  (119 other events, 675.7 us)
Sparse Core Ops, SparseCore 0:
  317.9 272.0 all-reduce.6
where the time goes:
time: 616 us; the launch traced here: 604 us
  waiting for transfers between devices  278 us (45%)
  local copies, waits for them, and re-layouts  182 us (30%)
  other arithmetic  74.3 us (12%)
  matrix products  31.2 us (5%)
  starting transfers between devices  20.5 us (3%)
  between operations  17.5 us (3%)
    psum x1, waiting for transfers between devices, shards(): lax.psum((grad_fine, grad_down, grad_coarse, grad_up), ('space', 'rep'))  270 us
    gather x52, local copies, waits for them, and re-layouts, assemble(): gathered = jnp.take(part_cells, jnp.maximum(source_ids, 0), axis=0)  51 us
    reshape x27, local copies, waits for them, and re-layouts, lattice_columns(): padded[:, :, a:a + side, c:c + side, e:e + side]  43.6 us
    unnamed x366, local copies, waits for them, and re-layouts  29.9 us
    ppermute x6, starting transfers between devices, passed_along(): return lax.ppermute(block, axis, route)  20.5 us
    select_n x26, other arithmetic, assemble(): jnp.where((source_ids >= 0)[:, None, None, None, None], gathered, jnp.zer...  16.6 us
    gather x27, other arithmetic  15.4 us
    dot_general x26, matrix products, shards(): jnp.einsum('bm,bcxyz->mcxyz', selector, piece, precision=lax.Precision.HI...  14.4 us
  transfers between devices with their start and end apart: 7, of which 4 were waited for; matrix products, arithmetic and copies ran while one was open for 7% of the time, Pallas kernels for 0%

commit v1 on v0

--- a/solution.py
+++ b/solution.py
@@ -214,7 +214,7 @@
 
     grad_fine, _ = lax.scan(fine_weights, jnp.zeros(w_fine.shape, f32), (pad_groups, delta_groups))
     grad_fine, grad_down, grad_coarse, grad_up = lax.psum(
-        (grad_fine, grad_down, grad_coarse, grad_up), ("space", "rep")
+        lax.psum((grad_fine, grad_down, grad_coarse, grad_up), "space"), "rep"
     )
     factor = 1.0 / math.sqrt(lax.axis_size("rep") * peer_count * block_count * EDGE**3)
     return (

time: 616 us -> 610 us (level)
  the two profiles are of different devices: /device:TPU:2 before, /device:TPU:1 now
where the time goes in v1:
time: 610 us; the launch traced here: 598 us
  waiting for transfers between devices  278 us (46%)
  local copies, waits for them, and re-layouts  182 us (30%)
  other arithmetic  74.2 us (12%)
  matrix products  31.1 us (5%)
  between operations  17.4 us (3%)
  starting transfers between devices  15.3 us (3%)
    psum x1, waiting for transfers between devices, shards(): lax.psum((grad_fine, grad_down, grad_coarse, grad_up), 'space')  235 us
    gather x52, local copies, waits for them, and re-layouts, assemble(): gathered = jnp.take(part_cells, jnp.maximum(source_ids, 0), axis=0)  51.1 us
    reshape x27, local copies, waits for them, and re-layouts, lattice_columns(): padded[:, :, a:a + side, c:c + side, e:e + side]  43.6 us
    psum x1, waiting for transfers between devices, shards(): lax.psum(lax.psum((grad_fine, grad_down, grad_coarse, grad_up), 'space'),...  33 us
    unnamed x366, local copies, waits for them, and re-layouts  29.9 us
    select_n x26, other arithmetic, assemble(): jnp.where((source_ids >= 0)[:, None, None, None, None], gathered, jnp.zer...  16.5 us
    gather x27, other arithmetic  15.4 us
    ppermute x6, starting transfers between devices, passed_along(): return lax.ppermute(block, axis, route)  15.2 us
  transfers between devices with their start and end apart: 8, of which 5 were waited for; matrix products, arithmetic and copies ran while one was open for 7% of the time, Pallas kernels for 0%

profile of v1, /device:TPU:1, one launch (start us, length us, event | category | flops | bytes accessed | tf_op | source)
XLA Modules:
  0.0 598.2 jit_solution(11975748412356442493)
XLA Ops:
  8.8 1.6 gather_fusion
  10.6 5.0 collective-permute-start
  42.6 2.0 concatenate.387
  47.7 3.0 copy.303
  50.7 3.9 copy.304
  57.3 2.5 pad_maximum_fusion
  81.5 1.6 gather_fusion.7
  83.1 1.6 gather_fusion.5
  86.2 1.6 gather_fusion.16
  93.5 1.7 gather_fusion.17
  104.6 3.2 fusion.228
  107.8 5.6 fusion.227
  113.3 2.0 copy.375
  115.4 2.0 copy.374
  117.4 2.0 copy.373
  119.4 2.0 copy.372
  122.4 2.1 copy.370
  124.5 2.0 copy.369
  129.8 2.0 copy.393
  132.8 2.1 copy.391
  134.9 2.0 copy.390
  136.9 2.0 copy.389
  138.9 2.0 copy.388
  140.9 2.0 copy.387
  144.0 2.0 copy.385
  146.0 2.0 copy.384
  148.0 2.0 copy.383
  150.0 2.0 copy.382
  152.0 2.0 copy.381
  157.7 1.7 constant_dynamic-update-slice_fusion.25
  159.4 1.7 constant_dynamic-update-slice_fusion.24
  161.1 1.7 constant_dynamic-update-slice_fusion.23
  179.9 4.4 multiply_convert_fusion
  188.8 4.7 collective-permute-start.2
  198.0 4.0 collective-permute-done.3
  261.8 3.1 concatenate.384
  269.3 1.9 fusion.80
  280.9 2.2 fusion.22
  284.1 2.2 fusion.27
  286.7 2.2 fusion.30
  297.0 5.8 collective-permute-done.4
  307.7 6.0 convolution_bitcast_fusion.2
  313.7 234.8 %all-reduce.9.cloned.1.call-done = (f32[64,1728]{1,0:T(8,128)}, f32[64,512]{1,0:T(8,128)}, f32[64,1728]{1,0:T(8,128)}, f32[64,512]{1,0:T(8,128)}) async-done(((f32[64,1728]{1,0:T(8,128)}, f32[64,512]{1,0:T(8,128)}, f32[64,1728]{1,0:T(8,128)}, f32[64,512]{1,0:T(8,128)}), (f32[64,1728]{1,0:T(8,128)}, f32[64,512]{1,0:T(8,128)}, f32[64,1728]{1,0:T(8,128)}, f32[64,512]{1,0:T(8,128)})) %all-reduce.9.cloned.1.call-update) | async-done | bytes 1146896 | tf_op jit(solution)/shard_map/psum | solution.py:217
  551.2 33.0 %all-reduce.11.cloned.1.call-done = (f32[64,1728]{1,0:T(8,128)}, f32[64,512]{1,0:T(8,128)}, f32[64,1728]{1,0:T(8,128)}, f32[64,512]{1,0:T(8,128)}) async-done(((f32[64,1728]{1,0:T(8,128)}, f32[64,512]{1,0:T(8,128)}, f32[64,1728]{1,0:T(8,128)}, f32[64,512]{1,0:T(8,128)}), (f32[64,1728]{1,0:T(8,128)}, f32[64,512]{1,0:T(8,128)}, f32[64,1728]{1,0:T(8,128)}, f32[64,512]{1,0:T(8,128)})) %all-reduce.11.cloned.1.call-update) | async-done | bytes 1146896 | tf_op jit(solution)/shard_map/psum | solution.py:216
  584.1 1.8 broadcast_multiply_fusion.1
  585.9 1.6 broadcast_multiply_fusion.3
  587.5 1.6 broadcast_multiply_fusion.2
  589.1 1.8 broadcast_multiply_fusion
  (734 shorter events, 197.1 us)
Async XLA Ops:
  7.2 257.7 %copy-start = (bf16[64,1728]{1,0:T(8,128)(2,1)S(1)}, bf16[64,1728]{1,0:T(8,128)(2,1)}, u32[]{:S(2)}) copy-start(bf16[64,1728]{1,0:T(8,128)(2,1)} %param.261) | copy-start | bytes 663556
  7.2 541.4 %all-reduce.9.cloned.1.call-start = ((), (), s32[]{:S(2)}) async-start(), calls=%async_computation | async-start | bytes 2359296 | tf_op jit(solution)/shard_map/psum | solution.py:217
  10.6 37.1 %collective-permute-start = (bf16[16,64,512]{2,1,0:T(8,128)(2,1)S(1)}, bf16[16,64,512]{2,1,0:T(8,128)(2,1)}, u32[]{:S(2)}, u32[]{:S(2)}) collective-permute-start(bf16[16,64,512]{2,1,0:T(8,128)(2,1)S(1)} %broadcast_select_fusion.1), channel_id=1, source_target_pairs={{0,2},{2,4},{4,6},{6,8},{8,10},{10,12},{12,14},{14,16},{16,18},{18... | collective-permute-start | bytes 3145736 | tf_op jit(solution)/shard_map/ppermute | solution.py:16
  17.4 33.4 %collective-permute-start.1 = (bf16[16,64,512]{2,1,0:T(8,128)(2,1)}, bf16[16,64,512]{2,1,0:T(8,128)(2,1)}, u32[]{:S(2)}, u32[]{:S(2)}) collective-permute-start(bf16[16,64,512]{2,1,0:T(8,128)(2,1)} %broadcast_select_fusion), channel_id=1, source_target_pairs={{2,0},{4,2},{6,4},{8,6},{10,8},{12,10},{14,12},{16,14},{18,16},{20... | collective-permute-start | bytes 3145736 | tf_op jit(solution)/shard_map/ppermute | solution.py:16
  18.7 22.5 %copy-start.150 = (s32[2]{0:T(128)}, s32[2]{0:T(128)S(1)}, u32[]{:S(2)}) copy-start(s32[2]{0:T(128)S(1)} %iota_multiply_fusion) | copy-start | bytes 28
  19.6 21.6 %copy-start.73 = (s32[4]{0:T(128)}, s32[4]{0:T(128)S(1)}, u32[]{:S(2)}) copy-start(s32[4]{0:T(128)S(1)} %get-tuple-element.1376) | copy-start | bytes 52
  22.6 18.6 %copy-start.43 = (s32[4]{0:T(128)}, s32[4]{0:T(128)S(1)}, u32[]{:S(2)}) copy-start(s32[4]{0:T(128)S(1)} %get-tuple-element.1356) | copy-start | bytes 52
  22.6 18.6 %copy-start.45 = (s32[4]{0:T(128)}, s32[4]{0:T(128)S(1)}, u32[]{:S(2)}) copy-start(s32[4]{0:T(128)S(1)} %get-tuple-element.1357) | copy-start | bytes 52
  22.6 18.6 %copy-start.47 = (s32[4]{0:T(128)}, s32[4]{0:T(128)S(1)}, u32[]{:S(2)}) copy-start(s32[4]{0:T(128)S(1)} %get-tuple-element.1359) | copy-start | bytes 52
  22.6 18.6 %copy-start.49 = (s32[4]{0:T(128)}, s32[4]{0:T(128)S(1)}, u32[]{:S(2)}) copy-start(s32[4]{0:T(128)S(1)} %get-tuple-element.1361) | copy-start | bytes 52
  22.6 18.6 %copy-start.107 = (s32[4]{0:T(128)}, s32[4]{0:T(128)S(1)}, u32[]{:S(2)}) copy-start(s32[4]{0:T(128)S(1)} %get-tuple-element.1352) | copy-start | bytes 52
  22.6 18.6 %copy-start.109 = (s32[4]{0:T(128)}, s32[4]{0:T(128)S(1)}, u32[]{:S(2)}) copy-start(s32[4]{0:T(128)S(1)} %get-tuple-element.1354) | copy-start | bytes 52
  22.6 18.6 %copy-start.111 = (s32[4]{0:T(128)}, s32[4]{0:T(128)S(1)}, u32[]{:S(2)}) copy-start(s32[4]{0:T(128)S(1)} %get-tuple-element.1358) | copy-start | bytes 52
  22.7 18.6 %copy-start.113 = (s32[4]{0:T(128)}, s32[4]{0:T(128)S(1)}, u32[]{:S(2)}) copy-start(s32[4]{0:T(128)S(1)} %get-tuple-element.1360) | copy-start | bytes 52
  22.7 25.0 %copy-start.51 = (s32[4]{0:T(128)}, s32[4]{0:T(128)S(1)}, u32[]{:S(2)}) copy-start(s32[4]{0:T(128)S(1)} %get-tuple-element.1362) | copy-start | bytes 52
  22.7 25.0 %copy-start.53 = (s32[4]{0:T(128)}, s32[4]{0:T(128)S(1)}, u32[]{:S(2)}) copy-start(s32[4]{0:T(128)S(1)} %get-tuple-element.1363) | copy-start | bytes 52
  22.7 25.0 %copy-start.55 = (s32[4]{0:T(128)}, s32[4]{0:T(128)S(1)}, u32[]{:S(2)}) copy-start(s32[4]{0:T(128)S(1)} %get-tuple-element.1364) | copy-start | bytes 52
  22.7 25.0 %copy-start.57 = (s32[4]{0:T(128)}, s32[4]{0:T(128)S(1)}, u32[]{:S(2)}) copy-start(s32[4]{0:T(128)S(1)} %get-tuple-element.1365) | copy-start | bytes 52
  22.7 25.0 %copy-start.59 = (s32[4]{0:T(128)}, s32[4]{0:T(128)S(1)}, u32[]{:S(2)}) copy-start(s32[4]{0:T(128)S(1)} %get-tuple-element.1366) | copy-start | bytes 52
  22.7 25.0 %copy-start.61 = (s32[4]{0:T(128)}, s32[4]{0:T(128)S(1)}, u32[]{:S(2)}) copy-start(s32[4]{0:T(128)S(1)} %get-tuple-element.1367) | copy-start | bytes 52
  22.7 25.0 %copy-start.63 = (s32[4]{0:T(128)}, s32[4]{0:T(128)S(1)}, u32[]{:S(2)}) copy-start(s32[4]{0:T(128)S(1)} %get-tuple-element.1368) | copy-start | bytes 52
  22.7 25.0 %copy-start.115 = (s32[4]{0:T(128)}, s32[4]{0:T(128)S(1)}, u32[]{:S(2)}) copy-start(s32[4]{0:T(128)S(1)} %get-tuple-element.1369) | copy-start | bytes 52
  93.5 10.3 %copy-start.134 = (pred[4]{0:T(512)(128)(4,1)S(1)}, pred[4]{0:T(512)(128)(4,1)}, u32[]{:S(2)}) copy-start(pred[4]{0:T(512)(128)(4,1)} %get-tuple-element.1596) | copy-start | bytes 16
  93.5 10.3 %copy-start.135 = (pred[4]{0:T(512)(128)(4,1)S(1)}, pred[4]{0:T(512)(128)(4,1)}, u32[]{:S(2)}) copy-start(pred[4]{0:T(512)(128)(4,1)} %get-tuple-element.1597) | copy-start | bytes 16
  132.8 10.1 %copy-start.8 = (bf16[4,64,8,8,8]{1,0,4,3,2:T(4,128)(2,1)S(1)}, bf16[4,64,8,8,8]{1,0,4,3,2:T(4,128)(2,1)}, u32[]{:S(2)}) copy-start(bf16[4,64,8,8,8]{1,0,4,3,2:T(4,128)(2,1)} %get-tuple-element.1451) | copy-start | bytes 786436
  144.0 10.1 %copy-start.7 = (bf16[4,64,8,8,8]{1,0,4,3,2:T(4,128)(2,1)S(1)}, bf16[4,64,8,8,8]{1,0,4,3,2:T(4,128)(2,1)}, u32[]{:S(2)}) copy-start(bf16[4,64,8,8,8]{1,0,4,3,2:T(4,128)(2,1)} %get-tuple-element.1457) | copy-start | bytes 786436
  185.0 9.8 %copy-start.158 = (s32[5]{0:T(128)S(1)}, s32[5]{0:T(128)}, u32[]{:S(2)}) copy-start(s32[5]{0:T(128)} %concatenate.387) | copy-start | bytes 64
  185.1 9.8 %copy-start.159 = (s32[5]{0:T(128)S(1)}, s32[5]{0:T(128)}, u32[]{:S(2)}) copy-start(s32[5]{0:T(128)} %constant.3474.clone.1) | copy-start | bytes 64
  185.1 10.4 %copy-start.12 = (bf16[1,4,64,512]{3,2,1,0:T(8,128)(2,1)S(1)}, bf16[1,4,64,512]{3,2,1,0:T(8,128)(2,1)}, u32[]{:S(2)}) copy-start(bf16[1,4,64,512]{3,2,1,0:T(8,128)(2,1)} %param.263) | copy-start | bytes 786436
  187.0 10.2 %copy-start.151 = (s32[2]{0:T(128)S(1)}, s32[2]{0:T(128)}, u32[]{:S(2)}) copy-start(s32[2]{0:T(128)} %copy-done.150) | copy-start | bytes 28
  187.0 10.2 %copy-start.156 = (s32[5]{0:T(128)S(1)}, s32[5]{0:T(128)}, u32[]{:S(2)}) copy-start(s32[5]{0:T(128)} %constant.3473.clone.1) | copy-start | bytes 64
  187.0 10.2 %copy-start.157 = (s32[5]{0:T(128)S(1)}, s32[5]{0:T(128)}, u32[]{:S(2)}) copy-start(s32[5]{0:T(128)} %constant.3471.clone.1) | copy-start | bytes 64
  188.8 9.2 %collective-permute-start.2 = (bf16[16,64,64]{1,2,0:T(8,128)(2,1)S(1)}, bf16[16,64,64]{1,2,0:T(8,128)(2,1)}, u32[]{:S(2)}, u32[]{:S(2)}) collective-permute-start(bf16[16,64,64]{1,2,0:T(8,128)(2,1)S(1)} %broadcast_select_fusion.3), channel_id=1, source_target_pairs={{0,2},{2,4},{4,6},{6,8},{8,10},{10,12},{12,14},{14,16},{16,18},{18... | collective-permute-start | bytes 393224 | tf_op jit(solution)/shard_map/ppermute | solution.py:16
  193.5 8.5 %collective-permute-start.3 = (bf16[16,64,64]{1,2,0:T(8,128)(2,1)}, bf16[16,64,64]{1,2,0:T(8,128)(2,1)}, u32[]{:S(2)}, u32[]{:S(2)}) collective-permute-start(bf16[16,64,64]{1,2,0:T(8,128)(2,1)} %broadcast_select_fusion.2), channel_id=1, source_target_pairs={{2,0},{4,2},{6,4},{8,6},{10,8},{12,10},{14,12},{16,14},{18,16},{20... | collective-permute-start | bytes 393224 | tf_op jit(solution)/shard_map/ppermute | solution.py:16
  203.9 16.9 %copy-start.153 = (pred[4]{0:T(512)(128)(4,1)S(1)}, pred[4]{0:T(512)(128)(4,1)}, u32[]{:S(2)}) copy-start(pred[4]{0:T(512)(128)(4,1)} %get-tuple-element.1633) | copy-start | bytes 16
  205.4 36.2 %copy-start.122 = (pred[4]{0:T(512)(128)(4,1)S(1)}, pred[4]{0:T(512)(128)(4,1)}, u32[]{:S(2)}) copy-start(pred[4]{0:T(512)(128)(4,1)} %get-tuple-element.1576) | copy-start | bytes 16
  205.7 37.4 %copy-start.118 = (pred[4]{0:T(512)(128)(4,1)S(1)}, pred[4]{0:T(512)(128)(4,1)}, u32[]{:S(2)}) copy-start(pred[4]{0:T(512)(128)(4,1)} %get-tuple-element.1580) | copy-start | bytes 16
  205.7 37.4 %copy-start.120 = (pred[4]{0:T(512)(128)(4,1)S(1)}, pred[4]{0:T(512)(128)(4,1)}, u32[]{:S(2)}) copy-start(pred[4]{0:T(512)(128)(4,1)} %get-tuple-element.1581) | copy-start | bytes 16
  242.3 13.4 %copy-start.96 = (pred[4]{0:T(512)(128)(4,1)S(1)}, pred[4]{0:T(512)(128)(4,1)}, u32[]{:S(2)}) copy-start(pred[4]{0:T(512)(128)(4,1)} %get-tuple-element.1560) | copy-start | bytes 16
  242.3 13.4 %copy-start.98 = (pred[4]{0:T(512)(128)(4,1)S(1)}, pred[4]{0:T(512)(128)(4,1)}, u32[]{:S(2)}) copy-start(pred[4]{0:T(512)(128)(4,1)} %get-tuple-element.1561) | copy-start | bytes 16
  244.7 11.9 %copy-start.86 = (pred[4]{0:T(512)(128)(4,1)S(1)}, pred[4]{0:T(512)(128)(4,1)}, u32[]{:S(2)}) copy-start(pred[4]{0:T(512)(128)(4,1)} %get-tuple-element.1636) | copy-start | bytes 16
  244.7 11.9 %copy-start.88 = (pred[4]{0:T(512)(128)(4,1)S(1)}, pred[4]{0:T(512)(128)(4,1)}, u32[]{:S(2)}) copy-start(pred[4]{0:T(512)(128)(4,1)} %get-tuple-element.1637) | copy-start | bytes 16
  290.6 12.2 %copy-start.154 = (s32[16]{0:T(128)S(1)}, s32[16]{0:T(128)}, u32[]{:S(2)}) copy-start(s32[16]{0:T(128)} %get-tuple-element.1526) | copy-start | bytes 196
  291.0 4.8 collective-permute-start.5
  293.4 12.5 %copy-start.36 = (bf16[64,512]{1,0:T(8,128)(2,1)S(1)}, bf16[64,512]{1,0:T(8,128)(2,1)}, u32[]{:S(2)}) copy-start(bf16[64,512]{1,0:T(8,128)(2,1)} %param.260) | copy-start | bytes 196612
  293.6 9.1 %collective-permute-start.4 = (bf16[16,1024]{0,1:T(8,128)(2,1)S(1)}, bf16[16,1024]{0,1:T(8,128)(2,1)S(1)}, u32[]{:S(2)}, u32[]{:S(2)}) collective-permute-start(bf16[16,1024]{0,1:T(8,128)(2,1)S(1)} %bitcast.1004), channel_id=1, source_target_pairs={{2,0},{4,2},{6,4},{8,6},{10,8},{12,10},{14,12},{16,14},{18,16},{20... | collective-permute-start | bytes 98312 | tf_op jit(solution)/shard_map/ppermute | solution.py:16
  313.6 234.9 %copy-start.37 = (bf16[64,512]{1,0:T(8,128)(2,1)S(1)}, bf16[64,512]{1,0:T(8,128)(2,1)}, u32[]{:S(2)}) copy-start(bf16[64,512]{1,0:T(8,128)(2,1)} %param.262) | copy-start | bytes 196612
  313.7 270.5 %all-reduce.11.cloned.1.call-start = ((), (), s32[]{:S(2)}) async-start(), calls=%async_computation.1 | async-start | bytes 2359296 | tf_op jit(solution)/shard_map/psum | solution.py:216
  (120 other events, 686.9 us)
Sparse Core Ops, SparseCore 0:
  313.8 234.7 all-reduce.8
  551.4 32.7 all-reduce.10
